TPU v7x, 128 devices: a whole 4x4x4 slice. The times are simulated.
128 devices in a mesh: row: 8 (over y, core), col: 16 (over x, z).
Axes of the slice: x: 4, y: 4, z: 4, core: 2. Of those that a mesh axis runs over, the one named last changes fastest.
Arguments:
- scores: float32 [32, 98304], P(None, ('row', 'col')), may hold values from -60 to 60
- tile_values: bfloat16 [8, 16, 480, 128, 128], P('row', 'col'), may hold values from 0 to 1
- tile_rows: int32 [8, 16, 480], P('row', 'col'), may hold values from 0 to 95, as said below
- tile_cols: int32 [8, 16, 480], P('row', 'col'), may hold values from 0 to 47, as said below
- tile_count: int32 [8, 16], P('row', 'col'), may hold values from 240 to 480, as said below
Outputs:
- solution: float32 [32, 98304], P(None, ('row', 'col'))
- residual: float32 [32, 98304], P(None, ('row', 'col'))
Inputs may be any that keep to these rules, and one draw needn't show every extreme that they name: `tile_rows`: on every device each local row tile is named by exactly 5 of the 480 slots. `tile_cols`: on every device each local column tile is named by exactly 10 of the slots. Only the first tile_count slots of a device are live; some device has all 480 slots live.
All inputs are finite; a program needn't handle non-finite values.
Results may differ from a plain program's by a relative error of at most 0.0031.
Values may be sent and summed in bfloat16 or wider, within the bound.
A program may use at most 128 MiB of HBM per device.

v0:
```python
import jax
import jax.numpy as jnp
from jax import lax
from jax.sharding import PartitionSpec as P

PER_ROW = 5
ITERS = 3
coupling = 0.2


def per_device(scores, tile_values, tile_rows, tile_cols, tile_count):
    tile_blocks = tile_values[0, 0]
    row_tile_ids = tile_rows[0, 0]
    col_tile_ids = tile_cols[0, 0]
    live_count = tile_count[0, 0]
    slot_count = tile_blocks.shape[0]
    tile_size = tile_blocks.shape[1]
    task_count = scores.shape[0]
    piece_len = scores.shape[1]
    row_span = piece_len * lax.axis_size("col")
    col_span = piece_len * lax.axis_size("row")
    row_tiles = row_span // tile_size
    col_tiles = col_span // tile_size
    block_slots = slot_count // PER_ROW
    live_mask = (jnp.arange(slot_count, dtype=jnp.int32) < live_count).astype(jnp.float32)
    row_weight = jnp.sum(tile_blocks, axis=2, dtype=jnp.float32) * live_mask[:, None]
    col_weight = jnp.sum(tile_blocks, axis=1, dtype=jnp.float32) * live_mask[:, None]
    row_degree_part = (
        jnp.zeros((row_tiles, tile_size), jnp.float32)
        .at[row_tile_ids]
        .add(row_weight)
        .reshape(1, row_span)
    )
    col_degree_part = (
        jnp.zeros((col_tiles, tile_size), jnp.float32)
        .at[col_tile_ids]
        .add(col_weight)
        .reshape(1, col_span)
    )

    def to_rows(partial_value):
        return lax.psum_scatter(partial_value, "col", scatter_dimension=1, tiled=True)

    def to_cols(partial_value):
        return lax.psum_scatter(partial_value, "row", scatter_dimension=1, tiled=True)

    degree = 0.5 * (to_rows(row_degree_part) + to_cols(col_degree_part))

    def inner_sums(parts):
        return lax.psum(parts, ("row", "col"))

    solution = jnp.zeros_like(scores)
    residual = scores
    direction = scores
    norm_now = inner_sums(jnp.sum(residual * residual, axis=1))
    for step_index in range(ITERS):
        graph_own_low = direction.astype(jnp.bfloat16)
        graph_col_dir = lax.all_gather(graph_own_low, "row", axis=1, tiled=True)
        graph_row_dir = lax.all_gather(graph_own_low, "col", axis=1, tiled=True)
        col_blocks = graph_col_dir.reshape(task_count, col_tiles, tile_size)
        row_blocks = graph_row_dir.reshape(task_count, row_tiles, tile_size)
        block_count = (live_count + block_slots - 1) // block_slots

        def one_block(block_index, totals):
            forward_sum, backward_sum = totals
            first_slot = block_index * block_slots
            tiles_here = lax.dynamic_slice_in_dim(tile_blocks, first_slot, block_slots, 0)
            rows_here = lax.dynamic_slice_in_dim(row_tile_ids, first_slot, block_slots, 0)
            cols_here = lax.dynamic_slice_in_dim(col_tile_ids, first_slot, block_slots, 0)
            live_here = (first_slot + jnp.arange(block_slots, dtype=jnp.int32) < live_count).astype(
                jnp.float32
            )
            col_pieces = jnp.take(col_blocks, cols_here, axis=1)
            row_pieces = jnp.take(row_blocks, rows_here, axis=1)
            forward = (
                jnp.einsum(
                    "ksd,sod->kso", col_pieces, tiles_here, preferred_element_type=jnp.float32
                )
                * live_here[None, :, None]
            )
            backward = (
                jnp.einsum(
                    "kso,sod->ksd", row_pieces, tiles_here, preferred_element_type=jnp.float32
                )
                * live_here[None, :, None]
            )
            return (
                forward_sum.at[:, rows_here, :].add(forward),
                backward_sum.at[:, cols_here, :].add(backward),
            )

        empty_sums = (
            jnp.zeros((task_count, row_tiles, tile_size), jnp.float32),
            jnp.zeros((task_count, col_tiles, tile_size), jnp.float32),
        )
        forward_sum, backward_sum = lax.fori_loop(0, block_count, one_block, empty_sums)
        forward_part = forward_sum.reshape(task_count, row_span)
        backward_part = backward_sum.reshape(task_count, col_span)
        image_field = direction + coupling * (
            degree * direction - 0.5 * (to_rows(forward_part) + to_cols(backward_part))
        )
        curvature = inner_sums(jnp.sum(direction * image_field, axis=1))
        step_size = norm_now / curvature
        solution = solution + step_size[:, None] * direction
        residual = residual - step_size[:, None] * image_field
        if step_index + 1 < ITERS:
            norm_next = inner_sums(jnp.sum(residual * residual, axis=1))
            direction = residual + (norm_next / norm_now)[:, None] * direction
            norm_now = norm_next
    return (solution, residual)


def solution(mesh):
    return jax.shard_map(
        per_device,
        mesh=mesh,
        in_specs=(
            P(None, ("row", "col")),
            P("row", "col", None, None, None),
            P("row", "col", None),
            P("row", "col", None),
            P("row", "col"),
        ),
        out_specs=(P(None, ("row", "col")), P(None, ("row", "col"))),
        check_vma=False,
    )
```

profile of v0, /device:TPU:1, one launch (start us, length us, event | category | flops | bytes accessed | tf_op | source)
XLA Modules:
  0.0 1218.0 jit_solution(540083142210740069)
XLA Ops:
  7.9 9.8 convert_reduce_fusion
  26.0 4.0 copy.53
  30.8 23.3 %all_gather.19 = bf16[32,12288]{1,0:T(8,128)(2,1)S(1)} all-gather(bf16[32,768]{1,0:T(8,128)(2,1)S(1)} %convert_element_type.43), channel_id=1, replica_groups=mesh['row'=8,'col'=16] {'col'}, dimensions={1}, use_global_device_ids=true | all-gather | bytes 835584 | tf_op jit(solution)/shard_map/all_gather | solution.py:59
  54.2 17.6 %all_gather.18 = bf16[32,6144]{1,0:T(8,128)(2,1)S(1)} all-gather(bf16[32,768]{1,0:T(8,128)(2,1)S(1)} %convert_element_type.43), channel_id=1, replica_groups=mesh['row'=8,'col'=16] {'row'}, dimensions={1}, use_global_device_ids=true | all-gather | bytes 442368 | tf_op jit(solution)/shard_map/all_gather | solution.py:58
  74.4 137.2 %while.36 = (s32[]{:T(128)}, f32[32,96,128]{2,0,1:T(8,128)}, f32[32,48,128]{2,0,1:T(8,128)S(1)}, s32[]{:T(128)}, s32[480]{0:T(512)}, /*index=5*/bf16[480,128,128...) while((s32[]{:T(128)}, f32[32,96,128]{2,0,1:T(8,128)}, ...), condition=%wide.region_11.14_spmd, body=%wide.region_8.13_spmd.sunk | while | flops 203689376 | bytes 23607144 | solution.py:96
  77.1 3.7 multiply_bitcast_fusion.12
  80.8 11.9 scatter_fusion
  97.4 4.4 scatter_fusion.1
  104.6 3.8 multiply_bitcast_fusion.12
  108.4 11.8 scatter_fusion
  125.0 4.5 scatter_fusion.1
  132.2 3.7 multiply_bitcast_fusion.12
  135.9 11.8 scatter_fusion
  152.5 4.4 scatter_fusion.1
  159.6 3.7 multiply_bitcast_fusion.12
  163.3 11.8 scatter_fusion
  179.8 4.4 scatter_fusion.1
  187.0 3.7 multiply_bitcast_fusion.12
  190.6 11.8 scatter_fusion
  207.2 4.4 scatter_fusion.1
  217.0 22.7 %reduce-scatter.15.cloned.1.call-done = f32[32,768]{1,0:T(8,128)} async-done(((f32[32,6144]{1,0:T(8,128)}), f32[32,768]{1,0:T(8,128)}) %reduce-scatter.15.cloned.1.call-update) | async-done | bytes 98320 | tf_op jit(solution)/shard_map/reduce_scatter | solution.py:45
  239.7 77.5 %reduce-scatter.13.cloned.1.call-done = f32[32,768]{1,0:T(8,128)} async-done(((f32[32,12288]{1,0:T(8,128)}), f32[32,768]{1,0:T(8,128)}) %reduce-scatter.13.cloned.1.call-update) | async-done | bytes 98320 | tf_op jit(solution)/shard_map/reduce_scatter | solution.py:42
  318.3 66.1 %all-reduce = (f32[32]{0:T(128)S(1)}, f32[32]{0:T(128)S(1)}) all-reduce(f32[32]{0:T(128)S(1)} %get-tuple-element.255, f32[32]{0:T(128)S(1)} %get-tuple-element.254), channel_id=1, replica_groups=mesh['row'=8,'col'=16] {'row','col'}, use_global_device_ids=true, to_apply=%region_1.0 | all-reduce | flops 64 | bytes 512 | tf_op jit(solution)/shard_map/psum | solution.py:50
  385.5 62.5 %psum.44 = f32[32]{0:T(128)S(1)} all-reduce(f32[32]{0:T(128)S(1)} %get-tuple-element.334), channel_id=1, replica_groups=mesh['row'=8,'col'=16] {'row','col'}, use_global_device_ids=true, to_apply=%region_17.20 | all-reduce | flops 32 | bytes 256 | tf_op jit(solution)/shard_map/psum | solution.py:50
  448.8 19.0 %all_gather.21 = bf16[32,12288]{1,0:T(8,128)(2,1)S(1)} all-gather(bf16[32,768]{1,0:T(8,128)(2,1)S(1)} %get-tuple-element.332), channel_id=1, replica_groups=mesh['row'=8,'col'=16] {'col'}, dimensions={1}, use_global_device_ids=true | all-gather | bytes 835584 | tf_op jit(solution)/shard_map/all_gather | solution.py:59
  467.8 18.5 %all_gather.20 = bf16[32,6144]{1,0:T(8,128)(2,1)S(1)} all-gather(bf16[32,768]{1,0:T(8,128)(2,1)S(1)} %get-tuple-element.332), channel_id=1, replica_groups=mesh['row'=8,'col'=16] {'row'}, dimensions={1}, use_global_device_ids=true | all-gather | bytes 442368 | tf_op jit(solution)/shard_map/all_gather | solution.py:58
  488.9 137.0 %while.37 = (s32[]{:T(128)}, f32[32,96,128]{2,0,1:T(8,128)}, f32[32,48,128]{2,0,1:T(8,128)S(1)}, s32[]{:T(128)}, s32[480]{0:T(512)}, /*index=5*/bf16[480,128,128...) while((s32[]{:T(128)}, f32[32,96,128]{2,0,1:T(8,128)}, ...), condition=%wide.region_21.24_spmd, body=%wide.region_18.23_spmd.sunk | while | flops 203689376 | bytes 23607556 | solution.py:96
  491.6 3.7 multiply_bitcast_fusion.14
  495.3 11.8 scatter_fusion.2
  511.8 4.4 scatter_fusion.3
  519.0 3.7 multiply_bitcast_fusion.14
  522.6 11.8 scatter_fusion.2
  539.2 4.5 scatter_fusion.3
  546.4 3.7 multiply_bitcast_fusion.14
  550.0 11.8 scatter_fusion.2
  566.6 4.4 scatter_fusion.3
  573.7 3.7 multiply_bitcast_fusion.14
  577.4 11.8 scatter_fusion.2
  594.0 4.4 scatter_fusion.3
  601.1 3.7 multiply_bitcast_fusion.14
  604.8 11.8 scatter_fusion.2
  621.4 4.4 scatter_fusion.3
  628.9 23.5 %reduce-scatter.19.cloned.1.call-done = f32[32,768]{1,0:T(8,128)} async-done(((f32[32,6144]{1,0:T(8,128)}), f32[32,768]{1,0:T(8,128)}) %reduce-scatter.19.cloned.1.call-update) | async-done | bytes 98320 | tf_op jit(solution)/shard_map/reduce_scatter | solution.py:45
  652.3 77.6 %reduce-scatter.17.cloned.1.call-done = f32[32,768]{1,0:T(8,128)} async-done(((f32[32,12288]{1,0:T(8,128)}), f32[32,768]{1,0:T(8,128)}) %reduce-scatter.17.cloned.1.call-update) | async-done | bytes 98320 | tf_op jit(solution)/shard_map/reduce_scatter | solution.py:42
  731.0 65.9 %psum.45 = f32[32]{0:T(128)S(1)} all-reduce(f32[32]{0:T(128)S(1)} %multiply_reduce_fusion.2), channel_id=1, replica_groups=mesh['row'=8,'col'=16] {'row','col'}, use_global_device_ids=true, to_apply=%region_25.28 | all-reduce | flops 32 | bytes 256 | tf_op jit(solution)/shard_map/psum | solution.py:50
  798.1 62.5 %psum.46 = f32[32]{0:T(128)S(1)} all-reduce(f32[32]{0:T(128)S(1)} %get-tuple-element.330), channel_id=1, replica_groups=mesh['row'=8,'col'=16] {'row','col'}, use_global_device_ids=true, to_apply=%region_27.30 | all-reduce | flops 32 | bytes 256 | tf_op jit(solution)/shard_map/psum | solution.py:50
  860.7 19.0 %all_gather.23 = bf16[32,12288]{1,0:T(8,128)(2,1)S(1)} all-gather(bf16[32,768]{1,0:T(8,128)(2,1)S(1)} %fusion.69), channel_id=1, replica_groups=mesh['row'=8,'col'=16] {'col'}, dimensions={1}, use_global_device_ids=true | all-gather | bytes 835584 | tf_op jit(solution)/shard_map/all_gather | solution.py:59
  879.7 18.8 %all_gather.22 = bf16[32,6144]{1,0:T(8,128)(2,1)S(1)} all-gather(bf16[32,768]{1,0:T(8,128)(2,1)S(1)} %fusion.69), channel_id=1, replica_groups=mesh['row'=8,'col'=16] {'row'}, dimensions={1}, use_global_device_ids=true | all-gather | bytes 442368 | tf_op jit(solution)/shard_map/all_gather | solution.py:58
  901.0 137.0 %while.38 = (s32[]{:T(128)}, f32[32,96,128]{2,0,1:T(8,128)}, f32[32,48,128]{2,0,1:T(8,128)S(1)}, s32[]{:T(128)}, s32[480]{0:T(512)}, /*index=5*/bf16[480,128,128...) while((s32[]{:T(128)}, f32[32,96,128]{2,0,1:T(8,128)}, ...), condition=%wide.region_31.34_spmd, body=%wide.region_28.33_spmd.sunk | while | flops 203689376 | bytes 23607556 | solution.py:96
  903.7 3.7 multiply_bitcast_fusion.16
  907.4 11.8 scatter_fusion.4
  924.0 4.4 scatter_fusion.5
  934.8 11.8 scatter_fusion.4
  951.3 4.5 scatter_fusion.5
  958.5 3.7 multiply_bitcast_fusion.16
  962.2 11.8 scatter_fusion.4
  978.7 4.4 scatter_fusion.5
  989.6 11.8 scatter_fusion.4
  1006.1 4.4 scatter_fusion.5
  1017.0 11.8 scatter_fusion.4
  1033.5 4.4 scatter_fusion.5
  1041.0 23.5 %reduce-scatter.23.cloned.1.call-done = f32[32,768]{1,0:T(8,128)} async-done(((f32[32,6144]{1,0:T(8,128)}), f32[32,768]{1,0:T(8,128)}) %reduce-scatter.23.cloned.1.call-update) | async-done | bytes 98320 | tf_op jit(solution)/shard_map/reduce_scatter | solution.py:45
  1064.5 77.8 %reduce-scatter.21.cloned.1.call-done = f32[32,768]{1,0:T(8,128)} async-done(((f32[32,12288]{1,0:T(8,128)}), f32[32,768]{1,0:T(8,128)}) %reduce-scatter.21.cloned.1.call-update) | async-done | bytes 98320 | tf_op jit(solution)/shard_map/reduce_scatter | solution.py:42
  1143.4 65.9 %psum.47 = f32[32]{0:T(128)S(1)} all-reduce(f32[32]{0:T(128)S(1)} %multiply_reduce_fusion), channel_id=1, replica_groups=mesh['row'=8,'col'=16] {'row','col'}, use_global_device_ids=true, to_apply=%region_35.38 | all-reduce | flops 32 | bytes 256 | tf_op jit(solution)/shard_map/psum | solution.py:50
  (231 shorter events, 158.3 us)
Async XLA Ops:
  7.2 207.5 %reduce-scatter.27.cloned.1.call-start = ((), (), s32[]{:S(2)}) async-start(), calls=%async_computation.15 | async-start | bytes 3538944
  22.9 192.9 %reduce-scatter.25.cloned.1.call-start = ((), (), s32[]{:S(2)}) async-start(), calls=%async_computation.14 | async-start | bytes 6684672
  29.9 0.9 copy-start.5
  30.0 209.8 %reduce-scatter.15.cloned.1.call-start = ((), (), s32[]{:S(2)}) async-start(), calls=%async_computation.9 | async-start | bytes 884736 | tf_op jit(solution)/shard_map/reduce_scatter | solution.py:45
  211.6 1.7 copy-start.1
  212.6 104.6 %reduce-scatter.13.cloned.1.call-start = ((), (), s32[]{:S(2)}) async-start(), calls=%async_computation.8 | async-start | bytes 1671168 | tf_op jit(solution)/shard_map/reduce_scatter | solution.py:42
  214.6 102.6 %copy-start.6 = (f32[32,768]{1,0:T(8,128)S(1)}, f32[32,768]{1,0:T(8,128)}, u32[]{:S(2)}) copy-start(f32[32,768]{1,0:T(8,128)} %param.15) | copy-start | bytes 294916
  214.6 437.7 %reduce-scatter.19.cloned.1.call-start = ((), (), s32[]{:S(2)}) async-start(), calls=%async_computation.11 | async-start | bytes 884736 | tf_op jit(solution)/shard_map/reduce_scatter | solution.py:45
  384.4 103.0 %copy-start.16 = (f32[32]{0:T(128)}, f32[32]{0:T(128)S(1)}, u32[]{:S(2)}) copy-start(f32[32]{0:T(128)S(1)} %div.22) | copy-start | bytes 388
  385.5 101.8 %copy-start.10 = (f32[32,768]{1,0:T(8,128)}, f32[32,768]{1,0:T(8,128)S(1)}, u32[]{:S(2)}) copy-start(f32[32,768]{1,0:T(8,128)S(1)} %get-tuple-element.335) | copy-start | bytes 294916
  448.0 39.3 %copy-start.20 = (f32[32]{0:T(128)}, f32[32]{0:T(128)S(1)}, u32[]{:S(2)}) copy-start(f32[32]{0:T(128)S(1)} %psum.44) | copy-start | bytes 388
  507.1 1.9 copy-start.12
  534.4 1.9 copy-start.12
  561.8 1.9 copy-start.12
  589.2 1.9 copy-start.12
  616.6 1.9 copy-start.12
  625.8 1.7 copy-start.2
  626.8 103.1 %reduce-scatter.17.cloned.1.call-start = ((), (), s32[]{:S(2)}) async-start(), calls=%async_computation.10 | async-start | bytes 1671168 | tf_op jit(solution)/shard_map/reduce_scatter | solution.py:42
  628.8 101.2 %copy-start.3 = (f32[32,768]{1,0:T(8,128)S(1)}, f32[32,768]{1,0:T(8,128)}, u32[]{:S(2)}) copy-start(f32[32,768]{1,0:T(8,128)} %get-tuple-element.333) | copy-start | bytes 294916
  628.8 168.1 %copy-start.21 = (f32[32]{0:T(128)S(1)}, f32[32]{0:T(128)}, u32[]{:S(2)}) copy-start(f32[32]{0:T(128)} %copy-done.20) | copy-start | bytes 388
  628.8 168.1 %copy-start.11 = (f32[32,768]{1,0:T(8,128)S(1)}, f32[32,768]{1,0:T(8,128)}, u32[]{:S(2)}) copy-start(f32[32,768]{1,0:T(8,128)} %copy-done.10) | copy-start | bytes 294916
  628.8 435.7 %reduce-scatter.23.cloned.1.call-start = ((), (), s32[]{:S(2)}) async-start(), calls=%async_computation.13 | async-start | bytes 884736 | tf_op jit(solution)/shard_map/reduce_scatter | solution.py:45
  796.9 102.6 %copy-start.18 = (f32[32]{0:T(128)}, f32[32]{0:T(128)S(1)}, u32[]{:S(2)}) copy-start(f32[32]{0:T(128)S(1)} %div.24) | copy-start | bytes 388
  798.1 101.5 %copy-start.8 = (f32[32,768]{1,0:T(8,128)}, f32[32,768]{1,0:T(8,128)S(1)}, u32[]{:S(2)}) copy-start(f32[32,768]{1,0:T(8,128)S(1)} %get-tuple-element.331) | copy-start | bytes 294916
  860.6 39.0 %copy-start.22 = (f32[32]{0:T(128)}, f32[32]{0:T(128)S(1)}, u32[]{:S(2)}) copy-start(f32[32]{0:T(128)S(1)} %psum.46) | copy-start | bytes 388
  860.6 39.0 %copy-start.14 = (f32[32]{0:T(128)}, f32[32]{0:T(128)S(1)}, u32[]{:S(2)}) copy-start(f32[32]{0:T(128)S(1)} %div.25) | copy-start | bytes 388
  919.2 1.9 copy-start.13
  946.6 1.9 copy-start.13
  974.0 1.9 copy-start.13
  1001.4 1.9 copy-start.13
  1028.8 1.9 copy-start.13
  1038.0 1.7 copy-start
  1039.0 103.3 %reduce-scatter.21.cloned.1.call-start = ((), (), s32[]{:S(2)}) async-start(), calls=%async_computation.12 | async-start | bytes 1671168 | tf_op jit(solution)/shard_map/reduce_scatter | solution.py:42
  1040.9 101.4 %copy-start.4 = (f32[32,768]{1,0:T(8,128)S(1)}, f32[32,768]{1,0:T(8,128)}, u32[]{:S(2)}) copy-start(f32[32,768]{1,0:T(8,128)} %get-tuple-element.333) | copy-start | bytes 294916
  1040.9 101.4 %copy-start.9 = (f32[32,768]{1,0:T(8,128)S(1)}, f32[32,768]{1,0:T(8,128)}, u32[]{:S(2)}) copy-start(f32[32,768]{1,0:T(8,128)} %copy-done.8) | copy-start | bytes 294916
  1040.9 101.4 %copy-start.15 = (f32[32]{0:T(128)S(1)}, f32[32]{0:T(128)}, u32[]{:S(2)}) copy-start(f32[32]{0:T(128)} %copy-done.14) | copy-start | bytes 388
  1040.9 168.4 %copy-start.23 = (f32[32]{0:T(128)S(1)}, f32[32]{0:T(128)}, u32[]{:S(2)}) copy-start(f32[32]{0:T(128)} %copy-done.22) | copy-start | bytes 388
  1041.0 168.4 %copy-start.7 = (f32[32,768]{1,0:T(8,128)S(1)}, f32[32,768]{1,0:T(8,128)}, u32[]{:S(2)}) copy-start(f32[32,768]{1,0:T(8,128)} %param.15) | copy-start | bytes 294916
  1041.0 168.4 %copy-start.17 = (f32[32]{0:T(128)S(1)}, f32[32]{0:T(128)}, u32[]{:S(2)}) copy-start(f32[32]{0:T(128)} %copy-done.16) | copy-start | bytes 388
  1041.0 168.4 %copy-start.19 = (f32[32]{0:T(128)S(1)}, f32[32]{0:T(128)}, u32[]{:S(2)}) copy-start(f32[32]{0:T(128)} %copy-done.18) | copy-start | bytes 388
Sparse Core Ops, SparseCore 0:
  23.1 36.3 reduce-scatter.26
  62.9 82.0 reduce-scatter.24
  212.7 26.9 reduce-scatter.14
  242.8 74.3 reduce-scatter.12
  626.9 25.3 reduce-scatter.18
  655.4 74.4 reduce-scatter.16
  1039.1 25.3 reduce-scatter.22
  1067.7 74.5 reduce-scatter.20
where the time goes:
time: 1230 us; the launch traced here: 1220 us
  blocking collectives  439 us (36%)
  waiting for transfers between devices  303 us (25%)
  other arithmetic  297 us (24%)
  matrix products  98.6 us (8%)
  local copies, waits for them, and re-layouts  64 us (5%)
  between operations  15.1 us (1%)
    psum x5, blocking collectives, inner_sums(): return lax.psum(parts, ('row', 'col'))  323 us
    reduce_scatter x3, waiting for transfers between devices, to_rows(): lax.psum_scatter(partial_value, 'col', scatter_dimension=1, tiled=True)  233 us
    scatter-add x15, other arithmetic, one_block(): forward_sum.at[:, rows_here, :].add(forward)  177 us
    reduce_scatter x3, waiting for transfers between devices, to_cols(): lax.psum_scatter(partial_value, 'row', scatter_dimension=1, tiled=True)  69.7 us
    scatter-add x15, other arithmetic, one_block(): backward_sum.at[:, cols_here, :].add(backward)  66.7 us
    all_gather x3, blocking collectives, per_device(): graph_row_dir = lax.all_gather(graph_own_low, 'col', axis=1, tiled=True)  61.4 us
    dot_general x15, matrix products, one_block(): jnp.einsum('ksd,sod->kso', col_pieces, tiles_here, preferred_element_type...  55.3 us
    all_gather x3, blocking collectives, per_device(): graph_col_dir = lax.all_gather(graph_own_low, 'row', axis=1, tiled=True)  54.9 us
  transfers between devices with their start and end apart: 8, of which 6 were waited for; matrix products, arithmetic and copies ran while one was open for 13% of the time, Pallas kernels for 0%

commit v1 on v0

--- a/solution.py
+++ b/solution.py
@@ -47,7 +47,7 @@
     degree = 0.5 * (to_rows(row_degree_part) + to_cols(col_degree_part))
 
     def inner_sums(parts):
-        return lax.psum(parts, ("row", "col"))
+        return lax.psum(lax.psum(parts, "row"), "col")
 
     solution = jnp.zeros_like(scores)
     residual = scores

time: 1230 us -> 1160 us (0.943)
  blocking collectives: 439 us -> 362 us
    psum x5 -> x10, blocking collectives: 323 us -> 233 us  [inner_sums(): return lax.psum(lax.psum(parts, 'row'), 'col')]
    all_gather x3, blocking collectives: 54.9 us -> 69.4 us  [per_device(): graph_col_dir = lax.all_gather(graph_own_low, 'row', axis=1, tiled=True)]
where the time goes in v1:
time: 1160 us; the launch traced here: 1140 us
  blocking collectives  362 us (31%)
  waiting for transfers between devices  303 us (26%)
  other arithmetic  297 us (26%)
  matrix products  98.6 us (8%)
  local copies, waits for them, and re-layouts  64 us (6%)
  between operations  15.1 us (1%)
    reduce_scatter x3, waiting for transfers between devices, to_rows(): lax.psum_scatter(partial_value, 'col', scatter_dimension=1, tiled=True)  233 us
    psum x10, blocking collectives, inner_sums(): return lax.psum(lax.psum(parts, 'row'), 'col')  233 us
    scatter-add x15, other arithmetic, one_block(): forward_sum.at[:, rows_here, :].add(forward)  177 us
    reduce_scatter x3, waiting for transfers between devices, to_cols(): lax.psum_scatter(partial_value, 'row', scatter_dimension=1, tiled=True)  69.8 us
    all_gather x3, blocking collectives, per_device(): graph_col_dir = lax.all_gather(graph_own_low, 'row', axis=1, tiled=True)  69.4 us
    scatter-add x15, other arithmetic, one_block(): backward_sum.at[:, cols_here, :].add(backward)  66.7 us
    all_gather x3, blocking collectives, per_device(): graph_row_dir = lax.all_gather(graph_own_low, 'col', axis=1, tiled=True)  59.7 us
    dot_general x15, matrix products, one_block(): jnp.einsum('ksd,sod->kso', col_pieces, tiles_here, preferred_element_type...  55.3 us
  transfers between devices with their start and end apart: 8, of which 6 were waited for; matrix products, arithmetic and copies ran while one was open for 13% of the time, Pallas kernels for 0%

profile of v1, /device:TPU:1, one launch (start us, length us, event | category | flops | bytes accessed | tf_op | source)
XLA Modules:
  0.0 1140.4 jit_solution(6509980160255825990)
XLA Ops:
  7.9 9.8 convert_reduce_fusion
  26.0 4.0 copy.53
  30.8 23.3 %all_gather.19 = bf16[32,12288]{1,0:T(8,128)(2,1)S(1)} all-gather(bf16[32,768]{1,0:T(8,128)(2,1)S(1)} %convert_element_type.43), channel_id=1, replica_groups=mesh['row'=8,'col'=16] {'col'}, dimensions={1}, use_global_device_ids=true | all-gather | bytes 835584 | tf_op jit(solution)/shard_map/all_gather | solution.py:59
  54.2 17.6 %all_gather.18 = bf16[32,6144]{1,0:T(8,128)(2,1)S(1)} all-gather(bf16[32,768]{1,0:T(8,128)(2,1)S(1)} %convert_element_type.43), channel_id=1, replica_groups=mesh['row'=8,'col'=16] {'row'}, dimensions={1}, use_global_device_ids=true | all-gather | bytes 442368 | tf_op jit(solution)/shard_map/all_gather | solution.py:58
  74.4 137.2 %while.36 = (s32[]{:T(128)}, f32[32,96,128]{2,0,1:T(8,128)}, f32[32,48,128]{2,0,1:T(8,128)S(1)}, s32[]{:T(128)}, s32[480]{0:T(512)}, /*index=5*/bf16[480,128,128...) while((s32[]{:T(128)}, f32[32,96,128]{2,0,1:T(8,128)}, ...), condition=%wide.region_12.15_spmd, body=%wide.region_9.14_spmd.sunk | while | flops 203689376 | bytes 23607144 | solution.py:96
  77.1 3.7 multiply_bitcast_fusion.12
  80.8 11.9 %scatter_fusion = f32[32,96,128]{2,0,1:T(8,128)} fusion(f32[32,96,128]{2,0,1:T(8,128)} %get-tuple-element.571, s32[96]{0:T(128)S(1)} %get-tuple-element.524, f32[96,32,128]{2,1,0:T(8,128)S(1)} %multiply_bitcast_fusion.12), kind=kCustom, calls=%fused_computation.6.clone.1 | custom fusion | flops 393216 | bytes 4718976 | tf_op jit(solution)/shard_map/while/body/scatter-add | solution.py:88
  97.4 4.4 scatter_fusion.1
  104.6 3.8 multiply_bitcast_fusion.12
  108.4 11.8 %scatter_fusion = f32[32,96,128]{2,0,1:T(8,128)} fusion(f32[32,96,128]{2,0,1:T(8,128)} %get-tuple-element.571, s32[96]{0:T(128)S(1)} %get-tuple-element.524, f32[96,32,128]{2,1,0:T(8,128)S(1)} %multiply_bitcast_fusion.12), kind=kCustom, calls=%fused_computation.6.clone.1 | custom fusion | flops 393216 | bytes 4718976 | tf_op jit(solution)/shard_map/while/body/scatter-add | solution.py:88
  125.0 4.5 scatter_fusion.1
  132.2 3.7 multiply_bitcast_fusion.12
  135.9 11.8 %scatter_fusion = f32[32,96,128]{2,0,1:T(8,128)} fusion(f32[32,96,128]{2,0,1:T(8,128)} %get-tuple-element.571, s32[96]{0:T(128)S(1)} %get-tuple-element.524, f32[96,32,128]{2,1,0:T(8,128)S(1)} %multiply_bitcast_fusion.12), kind=kCustom, calls=%fused_computation.6.clone.1 | custom fusion | flops 393216 | bytes 4718976 | tf_op jit(solution)/shard_map/while/body/scatter-add | solution.py:88
  152.5 4.4 scatter_fusion.1
  159.6 3.7 multiply_bitcast_fusion.12
  163.3 11.8 %scatter_fusion = f32[32,96,128]{2,0,1:T(8,128)} fusion(f32[32,96,128]{2,0,1:T(8,128)} %get-tuple-element.571, s32[96]{0:T(128)S(1)} %get-tuple-element.524, f32[96,32,128]{2,1,0:T(8,128)S(1)} %multiply_bitcast_fusion.12), kind=kCustom, calls=%fused_computation.6.clone.1 | custom fusion | flops 393216 | bytes 4718976 | tf_op jit(solution)/shard_map/while/body/scatter-add | solution.py:88
  179.8 4.4 scatter_fusion.1
  187.0 3.7 multiply_bitcast_fusion.12
  190.6 11.8 %scatter_fusion = f32[32,96,128]{2,0,1:T(8,128)} fusion(f32[32,96,128]{2,0,1:T(8,128)} %get-tuple-element.571, s32[96]{0:T(128)S(1)} %get-tuple-element.524, f32[96,32,128]{2,1,0:T(8,128)S(1)} %multiply_bitcast_fusion.12), kind=kCustom, calls=%fused_computation.6.clone.1 | custom fusion | flops 393216 | bytes 4718976 | tf_op jit(solution)/shard_map/while/body/scatter-add | solution.py:88
  207.2 4.4 scatter_fusion.1
  217.0 22.7 %reduce-scatter.15.cloned.1.call-done = f32[32,768]{1,0:T(8,128)} async-done(((f32[32,6144]{1,0:T(8,128)}), f32[32,768]{1,0:T(8,128)}) %reduce-scatter.15.cloned.1.call-update) | async-done | bytes 98320 | tf_op jit(solution)/shard_map/reduce_scatter | solution.py:45
  239.7 77.5 %reduce-scatter.13.cloned.1.call-done = f32[32,768]{1,0:T(8,128)} async-done(((f32[32,12288]{1,0:T(8,128)}), f32[32,768]{1,0:T(8,128)}) %reduce-scatter.13.cloned.1.call-update) | async-done | bytes 98320 | tf_op jit(solution)/shard_map/reduce_scatter | solution.py:42
  318.3 14.1 %all-reduce.1 = (f32[32]{0:T(128)S(1)}, f32[32]{0:T(128)S(1)}) all-reduce(f32[32]{0:T(128)S(1)} %get-tuple-element.255, f32[32]{0:T(128)S(1)} %get-tuple-element.254), channel_id=1, replica_groups=mesh['row'=8,'col'=16] {'row'}, use_global_device_ids=true, to_apply=%region_1.0 | all-reduce | flops 64 | bytes 512 | tf_op jit(solution)/shard_map/psum | solution.py:50
  332.4 31.1 %all-reduce = (f32[32]{0:T(128)S(1)}, f32[32]{0:T(128)S(1)}) all-reduce(f32[32]{0:T(128)S(1)} %get-tuple-element.318, f32[32]{0:T(128)S(1)} %get-tuple-element.319), channel_id=1, replica_groups=mesh['row'=8,'col'=16] {'col'}, use_global_device_ids=true, to_apply=%region_2.0 | all-reduce | flops 64 | bytes 512 | tf_op jit(solution)/shard_map/psum | solution.py:50
  364.7 19.9 %psum.88 = f32[32]{0:T(128)S(1)} all-reduce(f32[32]{0:T(128)S(1)} %get-tuple-element.336), channel_id=1, replica_groups=mesh['row'=8,'col'=16] {'row'}, use_global_device_ids=true, to_apply=%region_19.22 | all-reduce | flops 32 | bytes 256 | tf_op jit(solution)/shard_map/psum | solution.py:50
  384.6 28.5 %psum.89 = f32[32]{0:T(128)S(1)} all-reduce(f32[32]{0:T(128)S(1)} %psum.88), channel_id=1, replica_groups=mesh['row'=8,'col'=16] {'col'}, use_global_device_ids=true, to_apply=%region_20.23 | all-reduce | flops 32 | bytes 256 | tf_op jit(solution)/shard_map/psum | solution.py:50
  413.9 18.2 %all_gather.21 = bf16[32,12288]{1,0:T(8,128)(2,1)S(1)} all-gather(bf16[32,768]{1,0:T(8,128)(2,1)S(1)} %get-tuple-element.334), channel_id=1, replica_groups=mesh['row'=8,'col'=16] {'col'}, dimensions={1}, use_global_device_ids=true | all-gather | bytes 835584 | tf_op jit(solution)/shard_map/all_gather | solution.py:59
  432.1 25.9 %all_gather.20 = bf16[32,6144]{1,0:T(8,128)(2,1)S(1)} all-gather(bf16[32,768]{1,0:T(8,128)(2,1)S(1)} %get-tuple-element.334), channel_id=1, replica_groups=mesh['row'=8,'col'=16] {'row'}, dimensions={1}, use_global_device_ids=true | all-gather | bytes 442368 | tf_op jit(solution)/shard_map/all_gather | solution.py:58
  460.5 137.0 %while.37 = (s32[]{:T(128)}, f32[32,96,128]{2,0,1:T(8,128)}, f32[32,48,128]{2,0,1:T(8,128)S(1)}, s32[]{:T(128)}, s32[480]{0:T(512)}, /*index=5*/bf16[480,128,128...) while((s32[]{:T(128)}, f32[32,96,128]{2,0,1:T(8,128)}, ...), condition=%wide.region_24.27_spmd, body=%wide.region_21.26_spmd.sunk | while | flops 203689376 | bytes 23607556 | solution.py:96
  463.2 3.7 multiply_bitcast_fusion.14
  466.9 11.8 %scatter_fusion.2 = f32[32,96,128]{2,0,1:T(8,128)} fusion(f32[32,96,128]{2,0,1:T(8,128)} %get-tuple-element.613, s32[96]{0:T(128)S(1)} %get-tuple-element.538, f32[96,32,128]{2,1,0:T(8,128)S(1)} %multiply_bitcast_fusion.14), kind=kCustom, calls=%fused_computation.8.clone.1 | custom fusion | flops 393216 | bytes 4718976 | tf_op jit(solution)/shard_map/while/body/scatter-add | solution.py:88
  483.5 4.4 scatter_fusion.3
  490.6 3.7 multiply_bitcast_fusion.14
  494.3 11.8 %scatter_fusion.2 = f32[32,96,128]{2,0,1:T(8,128)} fusion(f32[32,96,128]{2,0,1:T(8,128)} %get-tuple-element.613, s32[96]{0:T(128)S(1)} %get-tuple-element.538, f32[96,32,128]{2,1,0:T(8,128)S(1)} %multiply_bitcast_fusion.14), kind=kCustom, calls=%fused_computation.8.clone.1 | custom fusion | flops 393216 | bytes 4718976 | tf_op jit(solution)/shard_map/while/body/scatter-add | solution.py:88
  510.9 4.5 scatter_fusion.3
  521.7 11.8 %scatter_fusion.2 = f32[32,96,128]{2,0,1:T(8,128)} fusion(f32[32,96,128]{2,0,1:T(8,128)} %get-tuple-element.613, s32[96]{0:T(128)S(1)} %get-tuple-element.538, f32[96,32,128]{2,1,0:T(8,128)S(1)} %multiply_bitcast_fusion.14), kind=kCustom, calls=%fused_computation.8.clone.1 | custom fusion | flops 393216 | bytes 4718976 | tf_op jit(solution)/shard_map/while/body/scatter-add | solution.py:88
  538.2 4.4 scatter_fusion.3
  549.1 11.8 %scatter_fusion.2 = f32[32,96,128]{2,0,1:T(8,128)} fusion(f32[32,96,128]{2,0,1:T(8,128)} %get-tuple-element.613, s32[96]{0:T(128)S(1)} %get-tuple-element.538, f32[96,32,128]{2,1,0:T(8,128)S(1)} %multiply_bitcast_fusion.14), kind=kCustom, calls=%fused_computation.8.clone.1 | custom fusion | flops 393216 | bytes 4718976 | tf_op jit(solution)/shard_map/while/body/scatter-add | solution.py:88
  565.6 4.4 scatter_fusion.3
  576.5 11.8 %scatter_fusion.2 = f32[32,96,128]{2,0,1:T(8,128)} fusion(f32[32,96,128]{2,0,1:T(8,128)} %get-tuple-element.613, s32[96]{0:T(128)S(1)} %get-tuple-element.538, f32[96,32,128]{2,1,0:T(8,128)S(1)} %multiply_bitcast_fusion.14), kind=kCustom, calls=%fused_computation.8.clone.1 | custom fusion | flops 393216 | bytes 4718976 | tf_op jit(solution)/shard_map/while/body/scatter-add | solution.py:88
  593.0 4.4 scatter_fusion.3
  600.5 23.6 %reduce-scatter.19.cloned.1.call-done = f32[32,768]{1,0:T(8,128)} async-done(((f32[32,6144]{1,0:T(8,128)}), f32[32,768]{1,0:T(8,128)}) %reduce-scatter.19.cloned.1.call-update) | async-done | bytes 98320 | tf_op jit(solution)/shard_map/reduce_scatter | solution.py:45
  624.1 77.6 %reduce-scatter.17.cloned.1.call-done = f32[32,768]{1,0:T(8,128)} async-done(((f32[32,12288]{1,0:T(8,128)}), f32[32,768]{1,0:T(8,128)}) %reduce-scatter.17.cloned.1.call-update) | async-done | bytes 98320 | tf_op jit(solution)/shard_map/reduce_scatter | solution.py:42
  702.7 14.1 %psum.90 = f32[32]{0:T(128)S(1)} all-reduce(f32[32]{0:T(128)S(1)} %multiply_reduce_fusion.2), channel_id=1, replica_groups=mesh['row'=8,'col'=16] {'row'}, use_global_device_ids=true, to_apply=%region_28.31 | all-reduce | flops 32 | bytes 256 | tf_op jit(solution)/shard_map/psum | solution.py:50
  716.8 31.2 %psum.91 = f32[32]{0:T(128)S(1)} all-reduce(f32[32]{0:T(128)S(1)} %psum.90), channel_id=1, replica_groups=mesh['row'=8,'col'=16] {'col'}, use_global_device_ids=true, to_apply=%region_29.32 | all-reduce | flops 32 | bytes 256 | tf_op jit(solution)/shard_map/psum | solution.py:50
  749.1 19.9 %psum.92 = f32[32]{0:T(128)S(1)} all-reduce(f32[32]{0:T(128)S(1)} %get-tuple-element.332), channel_id=1, replica_groups=mesh['row'=8,'col'=16] {'row'}, use_global_device_ids=true, to_apply=%region_31.34 | all-reduce | flops 32 | bytes 256 | tf_op jit(solution)/shard_map/psum | solution.py:50
  769.1 28.5 %psum.93 = f32[32]{0:T(128)S(1)} all-reduce(f32[32]{0:T(128)S(1)} %psum.92), channel_id=1, replica_groups=mesh['row'=8,'col'=16] {'col'}, use_global_device_ids=true, to_apply=%region_32.35 | all-reduce | flops 32 | bytes 256 | tf_op jit(solution)/shard_map/psum | solution.py:50
  797.6 18.1 %all_gather.23 = bf16[32,12288]{1,0:T(8,128)(2,1)S(1)} all-gather(bf16[32,768]{1,0:T(8,128)(2,1)S(1)} %fusion.69), channel_id=1, replica_groups=mesh['row'=8,'col'=16] {'col'}, dimensions={1}, use_global_device_ids=true | all-gather | bytes 835584 | tf_op jit(solution)/shard_map/all_gather | solution.py:59
  815.7 25.9 %all_gather.22 = bf16[32,6144]{1,0:T(8,128)(2,1)S(1)} all-gather(bf16[32,768]{1,0:T(8,128)(2,1)S(1)} %fusion.69), channel_id=1, replica_groups=mesh['row'=8,'col'=16] {'row'}, dimensions={1}, use_global_device_ids=true | all-gather | bytes 442368 | tf_op jit(solution)/shard_map/all_gather | solution.py:58
  844.2 137.0 %while.38 = (s32[]{:T(128)}, f32[32,96,128]{2,0,1:T(8,128)}, f32[32,48,128]{2,0,1:T(8,128)S(1)}, s32[]{:T(128)}, s32[480]{0:T(512)}, /*index=5*/bf16[480,128,128...) while((s32[]{:T(128)}, f32[32,96,128]{2,0,1:T(8,128)}, ...), condition=%wide.region_36.39_spmd, body=%wide.region_33.38_spmd.sunk | while | flops 203689376 | bytes 23607556 | solution.py:96
  850.6 11.8 %scatter_fusion.4 = f32[32,96,128]{2,0,1:T(8,128)} fusion(f32[32,96,128]{2,0,1:T(8,128)} %get-tuple-element.655, s32[96]{0:T(128)S(1)} %get-tuple-element.552, f32[96,32,128]{2,1,0:T(8,128)S(1)} %multiply_bitcast_fusion.16), kind=kCustom, calls=%fused_computation.10.clone.1 | custom fusion | flops 393216 | bytes 4718976 | tf_op jit(solution)/shard_map/while/body/scatter-add | solution.py:88
  867.1 4.4 scatter_fusion.5
  877.9 11.8 %scatter_fusion.4 = f32[32,96,128]{2,0,1:T(8,128)} fusion(f32[32,96,128]{2,0,1:T(8,128)} %get-tuple-element.655, s32[96]{0:T(128)S(1)} %get-tuple-element.552, f32[96,32,128]{2,1,0:T(8,128)S(1)} %multiply_bitcast_fusion.16), kind=kCustom, calls=%fused_computation.10.clone.1 | custom fusion | flops 393216 | bytes 4718976 | tf_op jit(solution)/shard_map/while/body/scatter-add | solution.py:88
  894.5 4.5 scatter_fusion.5
  905.3 11.8 %scatter_fusion.4 = f32[32,96,128]{2,0,1:T(8,128)} fusion(f32[32,96,128]{2,0,1:T(8,128)} %get-tuple-element.655, s32[96]{0:T(128)S(1)} %get-tuple-element.552, f32[96,32,128]{2,1,0:T(8,128)S(1)} %multiply_bitcast_fusion.16), kind=kCustom, calls=%fused_computation.10.clone.1 | custom fusion | flops 393216 | bytes 4718976 | tf_op jit(solution)/shard_map/while/body/scatter-add | solution.py:88
  921.9 4.4 scatter_fusion.5
  932.7 11.8 %scatter_fusion.4 = f32[32,96,128]{2,0,1:T(8,128)} fusion(f32[32,96,128]{2,0,1:T(8,128)} %get-tuple-element.655, s32[96]{0:T(128)S(1)} %get-tuple-element.552, f32[96,32,128]{2,1,0:T(8,128)S(1)} %multiply_bitcast_fusion.16), kind=kCustom, calls=%fused_computation.10.clone.1 | custom fusion | flops 393216 | bytes 4718976 | tf_op jit(solution)/shard_map/while/body/scatter-add | solution.py:88
  949.3 4.4 scatter_fusion.5
  960.1 11.8 %scatter_fusion.4 = f32[32,96,128]{2,0,1:T(8,128)} fusion(f32[32,96,128]{2,0,1:T(8,128)} %get-tuple-element.655, s32[96]{0:T(128)S(1)} %get-tuple-element.552, f32[96,32,128]{2,1,0:T(8,128)S(1)} %multiply_bitcast_fusion.16), kind=kCustom, calls=%fused_computation.10.clone.1 | custom fusion | flops 393216 | bytes 4718976 | tf_op jit(solution)/shard_map/while/body/scatter-add | solution.py:88
  976.7 4.4 scatter_fusion.5
  984.2 23.6 %reduce-scatter.23.cloned.1.call-done = f32[32,768]{1,0:T(8,128)} async-done(((f32[32,6144]{1,0:T(8,128)}), f32[32,768]{1,0:T(8,128)}) %reduce-scatter.23.cloned.1.call-update) | async-done | bytes 98320 | tf_op jit(solution)/shard_map/reduce_scatter | solution.py:45
  1007.7 77.7 %reduce-scatter.21.cloned.1.call-done = f32[32,768]{1,0:T(8,128)} async-done(((f32[32,12288]{1,0:T(8,128)}), f32[32,768]{1,0:T(8,128)}) %reduce-scatter.21.cloned.1.call-update) | async-done | bytes 98320 | tf_op jit(solution)/shard_map/reduce_scatter | solution.py:42
  1086.6 14.1 %psum.94 = f32[32]{0:T(128)S(1)} all-reduce(f32[32]{0:T(128)S(1)} %multiply_reduce_fusion), channel_id=1, replica_groups=mesh['row'=8,'col'=16] {'row'}, use_global_device_ids=true, to_apply=%region_40.43 | all-reduce | flops 32 | bytes 256 | tf_op jit(solution)/shard_map/psum | solution.py:50
  1100.7 31.2 %psum.95 = f32[32]{0:T(128)S(1)} all-reduce(f32[32]{0:T(128)S(1)} %psum.94), channel_id=1, replica_groups=mesh['row'=8,'col'=16] {'col'}, use_global_device_ids=true, to_apply=%region_41.44 | all-reduce | flops 32 | bytes 256 | tf_op jit(solution)/shard_map/psum | solution.py:50
  (236 shorter events, 176.7 us)
Async XLA Ops:
  7.2 207.5 %reduce-scatter.27.cloned.1.call-start = ((), (), s32[]{:S(2)}) async-start(), calls=%async_computation.15 | async-start | bytes 3538944
  22.9 192.9 %reduce-scatter.25.cloned.1.call-start = ((), (), s32[]{:S(2)}) async-start(), calls=%async_computation.14 | async-start | bytes 6684672
  29.9 0.9 copy-start.5
  30.0 209.8 %reduce-scatter.15.cloned.1.call-start = ((), (), s32[]{:S(2)}) async-start(), calls=%async_computation.9 | async-start | bytes 884736 | tf_op jit(solution)/shard_map/reduce_scatter | solution.py:45
  211.6 1.7 copy-start.1
  212.6 104.6 %reduce-scatter.13.cloned.1.call-start = ((), (), s32[]{:S(2)}) async-start(), calls=%async_computation.8 | async-start | bytes 1671168 | tf_op jit(solution)/shard_map/reduce_scatter | solution.py:42
  214.6 102.6 %copy-start.6 = (f32[32,768]{1,0:T(8,128)S(1)}, f32[32,768]{1,0:T(8,128)}, u32[]{:S(2)}) copy-start(f32[32,768]{1,0:T(8,128)} %param.15) | copy-start | bytes 294916
  214.6 409.5 %reduce-scatter.19.cloned.1.call-start = ((), (), s32[]{:S(2)}) async-start(), calls=%async_computation.11 | async-start | bytes 884736 | tf_op jit(solution)/shard_map/reduce_scatter | solution.py:45
  363.6 95.4 %copy-start.16 = (f32[32]{0:T(128)}, f32[32]{0:T(128)S(1)}, u32[]{:S(2)}) copy-start(f32[32]{0:T(128)S(1)} %div.22) | copy-start | bytes 388
  364.7 94.3 %copy-start.10 = (f32[32,768]{1,0:T(8,128)}, f32[32,768]{1,0:T(8,128)S(1)}, u32[]{:S(2)}) copy-start(f32[32,768]{1,0:T(8,128)S(1)} %get-tuple-element.337) | copy-start | bytes 294916
  413.1 45.9 %copy-start.20 = (f32[32]{0:T(128)}, f32[32]{0:T(128)S(1)}, u32[]{:S(2)}) copy-start(f32[32]{0:T(128)S(1)} %psum.89) | copy-start | bytes 388
  478.7 1.9 copy-start.12
  506.1 1.9 copy-start.12
  533.5 1.9 copy-start.12
  560.9 1.9 copy-start.12
  588.3 1.9 copy-start.12
  597.5 1.7 copy-start.2
  598.5 103.2 %reduce-scatter.17.cloned.1.call-start = ((), (), s32[]{:S(2)}) async-start(), calls=%async_computation.10 | async-start | bytes 1671168 | tf_op jit(solution)/shard_map/reduce_scatter | solution.py:42
  600.4 101.2 %copy-start.3 = (f32[32,768]{1,0:T(8,128)S(1)}, f32[32,768]{1,0:T(8,128)}, u32[]{:S(2)}) copy-start(f32[32,768]{1,0:T(8,128)} %get-tuple-element.335) | copy-start | bytes 294916
  600.5 147.5 %copy-start.21 = (f32[32]{0:T(128)S(1)}, f32[32]{0:T(128)}, u32[]{:S(2)}) copy-start(f32[32]{0:T(128)} %copy-done.20) | copy-start | bytes 388
  600.5 147.5 %copy-start.11 = (f32[32,768]{1,0:T(8,128)S(1)}, f32[32,768]{1,0:T(8,128)}, u32[]{:S(2)}) copy-start(f32[32,768]{1,0:T(8,128)} %copy-done.10) | copy-start | bytes 294916
  600.5 407.2 %reduce-scatter.23.cloned.1.call-start = ((), (), s32[]{:S(2)}) async-start(), calls=%async_computation.13 | async-start | bytes 884736 | tf_op jit(solution)/shard_map/reduce_scatter | solution.py:45
  748.0 94.6 %copy-start.18 = (f32[32]{0:T(128)}, f32[32]{0:T(128)S(1)}, u32[]{:S(2)}) copy-start(f32[32]{0:T(128)S(1)} %div.24) | copy-start | bytes 388
  749.1 93.6 %copy-start.8 = (f32[32,768]{1,0:T(8,128)}, f32[32,768]{1,0:T(8,128)S(1)}, u32[]{:S(2)}) copy-start(f32[32,768]{1,0:T(8,128)S(1)} %get-tuple-element.333) | copy-start | bytes 294916
  797.5 45.2 %copy-start.22 = (f32[32]{0:T(128)}, f32[32]{0:T(128)S(1)}, u32[]{:S(2)}) copy-start(f32[32]{0:T(128)S(1)} %psum.93) | copy-start | bytes 388
  797.5 45.2 %copy-start.14 = (f32[32]{0:T(128)}, f32[32]{0:T(128)S(1)}, u32[]{:S(2)}) copy-start(f32[32]{0:T(128)S(1)} %div.25) | copy-start | bytes 388
  862.4 1.9 copy-start.13
  889.7 1.9 copy-start.13
  917.1 1.9 copy-start.13
  944.5 1.9 copy-start.13
  971.9 1.9 copy-start.13
  981.1 1.7 copy-start
  982.1 103.3 %reduce-scatter.21.cloned.1.call-start = ((), (), s32[]{:S(2)}) async-start(), calls=%async_computation.12 | async-start | bytes 1671168 | tf_op jit(solution)/shard_map/reduce_scatter | solution.py:42
  984.1 101.3 %copy-start.4 = (f32[32,768]{1,0:T(8,128)S(1)}, f32[32,768]{1,0:T(8,128)}, u32[]{:S(2)}) copy-start(f32[32,768]{1,0:T(8,128)} %get-tuple-element.335) | copy-start | bytes 294916
  984.1 101.3 %copy-start.9 = (f32[32,768]{1,0:T(8,128)S(1)}, f32[32,768]{1,0:T(8,128)}, u32[]{:S(2)}) copy-start(f32[32,768]{1,0:T(8,128)} %copy-done.8) | copy-start | bytes 294916
  984.1 101.3 %copy-start.15 = (f32[32]{0:T(128)S(1)}, f32[32]{0:T(128)}, u32[]{:S(2)}) copy-start(f32[32]{0:T(128)} %copy-done.14) | copy-start | bytes 388
  984.1 147.7 %copy-start.23 = (f32[32]{0:T(128)S(1)}, f32[32]{0:T(128)}, u32[]{:S(2)}) copy-start(f32[32]{0:T(128)} %copy-done.22) | copy-start | bytes 388
  984.1 147.7 %copy-start.7 = (f32[32,768]{1,0:T(8,128)S(1)}, f32[32,768]{1,0:T(8,128)}, u32[]{:S(2)}) copy-start(f32[32,768]{1,0:T(8,128)} %param.15) | copy-start | bytes 294916
  984.1 147.7 %copy-start.17 = (f32[32]{0:T(128)S(1)}, f32[32]{0:T(128)}, u32[]{:S(2)}) copy-start(f32[32]{0:T(128)} %copy-done.16) | copy-start | bytes 388
  984.1 147.7 %copy-start.19 = (f32[32]{0:T(128)S(1)}, f32[32]{0:T(128)}, u32[]{:S(2)}) copy-start(f32[32]{0:T(128)} %copy-done.18) | copy-start | bytes 388
Sparse Core Ops, SparseCore 0:
  23.1 36.3 reduce-scatter.26
  62.9 82.0 reduce-scatter.24
  212.7 26.9 reduce-scatter.14
  242.8 74.3 reduce-scatter.12
  598.6 25.4 reduce-scatter.18
  627.2 74.4 reduce-scatter.16
  982.2 25.4 reduce-scatter.22
  1010.9 74.4 reduce-scatter.20
